TPU v7x, 32 devices: a whole 2x2x4 slice. The times are simulated.
32 devices in a mesh: sp: 2 (over x), fsdp: 16 (over z, y, core).
Axes of the slice: x: 2, y: 2, z: 4, core: 2. Of those that a mesh axis runs over, the one named last changes fastest.
Arguments:
- tokens: bfloat16 [16, 1024, 1024], P('fsdp', 'sp'), may hold values from -6 to 6
- segments: int32 [16, 1024], P('fsdp', 'sp'), may hold values from 0 to 7, never falling along the last dimension, each value on 1 to 256 neighbouring positions
- cotangent: bfloat16 [16, 1024, 1024], P('fsdp', 'sp'), may hold values from -6 to 6
- gain_attn: bfloat16 [1024], P('fsdp'), may hold values from 0.5 to 1.5
- w_fac: bfloat16 [1024, 800], P('fsdp'), may hold values from -0.25 to 0.25
- w_out: bfloat16 [1024, 1024], P('fsdp'), may hold values from -0.75 to 0.75
- gain_ffn: bfloat16 [1024], P('fsdp'), may hold values from 0.5 to 1.5
- w_gu: bfloat16 [1024, 5632], P('fsdp'), may hold values from -0.1875 to 0.1875
- w_down: bfloat16 [2816, 1024], P('fsdp'), may hold values from -0.109375 to 0.109375
Outputs:
- out: bfloat16 [16, 1024, 1024], P('fsdp', 'sp')
- grad_tokens: float32 [16, 1024, 1024], P('fsdp', 'sp')
- grad_gain_attn: float32 [1024], P('fsdp')
- grad_w_fac: float32 [1024, 800], P('fsdp')
- grad_w_out: float32 [1024, 1024], P('fsdp')
- grad_gain_ffn: float32 [1024], P('fsdp')
- grad_w_gu: float32 [1024, 5632], P('fsdp')
- grad_w_down: float32 [2816, 1024], P('fsdp')
Inputs may be any that keep to these rules, and one draw needn't show every extreme that they name: `segments`: each row of 1024 numbers never falls and uses all 8 document numbers; a document has at most 256 tokens, and one of each row has exactly that many.
All inputs are finite; a program needn't handle non-finite values.
Results may differ from a plain program's by a relative error of at most 0.023.
Values may be sent and summed in bfloat16 or wider, within the bound.
A program may use at most 192 MiB of HBM per device.

v0:
```python
import functools

import jax
import jax.numpy as jnp
from jax import lax
from jax.experimental import pallas as pl
from jax.experimental.pallas import tpu as pltpu
from jax.sharding import PartitionSpec as P


H = 16
DH = 64
RQ = 6
RK = 2
FF = 2816
LANES = 128
NB = (RQ + 2 * RK) * DH
RANKS = RQ + 2 * RK

EPSILON = 1e-06
NEG = -1e30
F32 = jnp.float32
BF16 = jnp.bfloat16


def rms_norm(values, gain_row):
    factor = lax.rsqrt(jnp.mean(values * values, axis=-1, keepdims=True) + EPSILON)
    return values * factor * gain_row


def swiglu(gate_up):
    return jax.nn.silu(gate_up[:, :FF]) * gate_up[:, FF:]


def product(left, right):
    return jnp.dot(left, right, preferred_element_type=F32)


def weight_grad(left, right):
    return jnp.einsum("ta,tb->ab", left, right, preferred_element_type=F32)


def back_product(grad_rows, weight):
    return jnp.einsum("tb,ab->ta", grad_rows, weight, preferred_element_type=F32)


def dot_nt(a, b):
    return lax.dot_general(a, b, (((1,), (1,)), ((), ())), preferred_element_type=F32)


def dot_tn(a, b):
    return lax.dot_general(a, b, (((0,), (0,)), ((), ())), preferred_element_type=F32)


def band_start(index, block, width):
    return pl.multiple_of(jnp.maximum(index * block - (width - block), 0), LANES)


def band_bias(index, start, seg_col, seg_row, block, width):
    rows = index * block + lax.broadcasted_iota(jnp.int32, (block, width), 0)
    cols = start + lax.broadcasted_iota(jnp.int32, (block, width), 1)
    keep = (seg_col == seg_row) & (cols <= rows)
    return jnp.where(keep, 0.0, NEG)


def half_masks(scale):
    lane = lax.broadcasted_iota(jnp.int32, (1, LANES), 1)
    low = jnp.where(lane < DH, scale, 0.0).astype(BF16)
    high = jnp.where(lane < DH, 0.0, scale).astype(BF16)
    return low, high


def split_pair(values, masks):
    return jnp.concatenate([values * masks[0], values * masks[1]], axis=0)


def attend_forward_kernel(q_ref, k_ref, v_ref, segc_ref, segr_ref, o_ref, *, block, width):
    index = pl.program_id(0)
    start = band_start(index, block, width)
    bias = band_bias(index, start, segc_ref[...], segr_ref[:, pl.ds(start, width)], block, width)
    bias = jnp.concatenate([bias, bias], axis=0)
    masks = half_masks(DH ** (-0.5))
    first = lax.broadcasted_iota(jnp.int32, (block, LANES), 1) < DH
    for pair in range(q_ref.shape[1] // LANES):
        lanes = slice(pair * LANES, (pair + 1) * LANES)
        queries = split_pair(q_ref[:, lanes], masks)
        keys = k_ref[pl.ds(start, width), lanes]
        values = v_ref[pl.ds(start, width), lanes]
        scores = dot_nt(queries, keys) + bias
        exponent = jnp.exp(scores - jnp.max(scores, axis=-1, keepdims=True))
        inverse = 1.0 / jnp.sum(exponent, axis=-1, keepdims=True)
        probs = (exponent * inverse).astype(BF16)
        mixed = product(probs, values)
        o_ref[:, lanes] = jnp.where(first, mixed[:block], mixed[block:]).astype(BF16)


def attend_backward_kernel(
    q_ref, k_ref, v_ref, g_ref, segc_ref, segr_ref, dq_ref, dk_ref, dv_ref, dk_acc, dv_acc,
    *, block, width
):
    index = pl.program_id(0)
    start = band_start(index, block, width)
    scaling = DH ** (-0.5)

    @pl.when(index == 0)
    def _():
        dk_acc[...] = jnp.zeros_like(dk_acc)
        dv_acc[...] = jnp.zeros_like(dv_acc)

    bias = band_bias(index, start, segc_ref[...], segr_ref[:, pl.ds(start, width)], block, width)
    bias = jnp.concatenate([bias, bias], axis=0)
    scale_masks = half_masks(scaling)
    unit_masks = half_masks(1.0)
    first = lax.broadcasted_iota(jnp.int32, (block, LANES), 1) < DH
    window = pl.ds(start, width)
    for pair in range(q_ref.shape[1] // LANES):
        lanes = slice(pair * LANES, (pair + 1) * LANES)
        queries = split_pair(q_ref[:, lanes], scale_masks)
        grads = split_pair(g_ref[:, lanes], unit_masks)
        keys = k_ref[window, lanes]
        values = v_ref[window, lanes]
        scores = dot_nt(queries, keys) + bias
        exponent = jnp.exp(scores - jnp.max(scores, axis=-1, keepdims=True))
        inverse = 1.0 / jnp.sum(exponent, axis=-1, keepdims=True)
        probs = exponent * inverse
        grad_probs = dot_nt(grads, values)
        inner = jnp.sum(probs * grad_probs, axis=-1, keepdims=True)
        grad_scores = (probs * (grad_probs - inner)).astype(BF16)
        grad_q = product(grad_scores, keys) * scaling
        dq_ref[:, lanes] = jnp.where(first, grad_q[:block], grad_q[block:]).astype(BF16)
        dk_acc[window, lanes] += dot_tn(grad_scores, queries)
        dv_acc[window, lanes] += dot_tn(probs.astype(BF16), grads)

    @pl.when(index == pl.num_programs(0) - 1)
    def _():
        dk_ref[...] = dk_acc[...].astype(BF16)
        dv_ref[...] = dv_acc[...].astype(BF16)


def attention_specs(length, columns):
    block = LANES
    width = min(length // 4 + block, length)
    whole = pl.BlockSpec((length, columns), lambda i: (0, 0))
    rows = pl.BlockSpec((block, columns), lambda i: (i, 0))
    seg_col = pl.BlockSpec((block, 1), lambda i: (i, 0))
    seg_row = pl.BlockSpec((1, length), lambda i: (0, 0))
    return block, width, whole, rows, seg_col, seg_row


def attend_forward(queries, keys, values, seg_all):
    length, columns = queries.shape
    block, width, whole, rows, seg_col, seg_row = attention_specs(length, columns)
    work = length * width * columns
    return pl.pallas_call(
        functools.partial(attend_forward_kernel, block=block, width=width),
        grid=(length // block,),
        in_specs=[rows, whole, whole, seg_col, seg_row],
        out_specs=rows,
        out_shape=jax.ShapeDtypeStruct((length, columns), BF16),
        cost_estimate=pl.CostEstimate(
            flops=16 * work, bytes_accessed=8 * length * columns, transcendentals=work // DH
        ),
        name="attend_forward",
    )(queries, keys, values, seg_all.reshape(length, 1), seg_all.reshape(1, length))


def attend_backward(queries, keys, values, grads, seg_all):
    length, columns = queries.shape
    block, width, whole, rows, seg_col, seg_row = attention_specs(length, columns)
    work = length * width * columns
    shape = jax.ShapeDtypeStruct((length, columns), BF16)
    return pl.pallas_call(
        functools.partial(attend_backward_kernel, block=block, width=width),
        grid=(length // block,),
        in_specs=[rows, whole, whole, rows, seg_col, seg_row],
        out_specs=[rows, whole, whole],
        out_shape=[shape, shape, shape],
        scratch_shapes=[pltpu.VMEM((length, columns), F32), pltpu.VMEM((length, columns), F32)],
        cost_estimate=pl.CostEstimate(
            flops=40 * work, bytes_accessed=14 * length * columns, transcendentals=work // DH
        ),
        name="attend_backward",
    )(queries, keys, values, grads, seg_all.reshape(length, 1), seg_all.reshape(1, length))


def expansion(heads):
    rows = lax.broadcasted_iota(jnp.int32, (2 * LANES, RANKS * heads * DH), 0) % LANES
    cols = lax.broadcasted_iota(jnp.int32, (2 * LANES, RANKS * heads * DH), 1)
    rank, head = cols // (heads * DH), (cols % (heads * DH)) // DH
    in_k = heads * RQ + head * RK + rank - RQ
    in_v = heads * (RQ + RK) + head * RK + rank - RQ - RK
    source = jnp.where(
        rank < RQ, head * RQ + rank, jnp.where(rank < RQ + RK, in_k, in_v)
    )
    return (rows == source).astype(BF16)


def high_low(values):
    high = values.astype(BF16)
    return high, (values - high.astype(F32)).astype(BF16)


def doubled(factor, rank, first):
    pair = factor[:, (rank // 2) * LANES : (rank // 2 + 1) * LANES]
    turned = pltpu.roll(pair, DH, 1)
    return jnp.where(first, pair, turned) if rank % 2 == 0 else jnp.where(first, turned, pair)


GROUPS = ((0, RQ), (RQ, RK), (RQ + RK, RK))


def heads_forward_kernel(x_ref, gain_ref, w_ref, e_ref, f_ref, q_ref, k_ref, v_ref):
    normed = rms_norm(x_ref[...].astype(F32), gain_ref[...]).astype(BF16)
    factor = product(normed, w_ref[...])
    f_ref[...] = factor
    spread = jnp.concatenate(high_low(factor[:, NB:]), axis=1)
    rows, columns = q_ref.shape
    first = lax.broadcasted_iota(jnp.int32, (rows, LANES), 1) < DH
    for (base, ranks), out_ref in zip(GROUPS, (q_ref, k_ref, v_ref)):
        total = None
        for rank in range(base, base + ranks):
            left = product(spread, e_ref[:, rank * columns : (rank + 1) * columns])
            right = jnp.concatenate([doubled(factor, rank, first)] * (columns // LANES), axis=1)
            total = left * right if total is None else total + left * right
        out_ref[...] = (total * (1.0 / ranks)).astype(BF16)


def heads_backward_kernel(f_ref, e_ref, dq_ref, dk_ref, dv_ref, g_ref):
    factor = f_ref[...]
    spread = jnp.concatenate(high_low(factor[:, NB:]), axis=1)
    rows, columns = dq_ref.shape
    first = lax.broadcasted_iota(jnp.int32, (rows, LANES), 1) < DH
    left_total = jnp.zeros((rows, LANES), F32)
    folded = []
    for (base, ranks), grad_ref in zip(GROUPS, (dq_ref, dk_ref, dv_ref)):
        grad = grad_ref[...].astype(F32) * (1.0 / ranks)
        for rank in range(base, base + ranks):
            ones = e_ref[:, rank * columns : (rank + 1) * columns]
            weighted = product(spread, ones) * grad
            right_grad = weighted[:, :LANES]
            for chunk in range(1, columns // LANES):
                right_grad = right_grad + weighted[:, chunk * LANES : (chunk + 1) * LANES]
            folded.append(right_grad + pltpu.roll(right_grad, DH, 1))
            right = jnp.concatenate([doubled(factor, rank, first)] * (columns // LANES), axis=1)
            high, low = high_low(grad * right)
            left_total = left_total + dot_nt(high, ones[:LANES]) + dot_nt(low, ones[:LANES])
    for pair in range(RANKS // 2):
        g_ref[:, pair * LANES : (pair + 1) * LANES] = jnp.where(
            first, folded[2 * pair], folded[2 * pair + 1]
        ).astype(BF16)
    g_ref[:, NB:] = left_total.astype(BF16)


HEAD_ROWS = 256


def heads_forward(tokens, gain_row, weights, spreader, columns):
    length, width = tokens.shape
    rows = min(HEAD_ROWS, length)
    block = lambda n: pl.BlockSpec((rows, n), lambda i: (i, 0))
    fixed = lambda a: pl.BlockSpec(a.shape, lambda i: (0, 0))
    head = jax.ShapeDtypeStruct((length, columns), BF16)
    return pl.pallas_call(
        heads_forward_kernel,
        grid=(length // rows,),
        in_specs=[block(width), fixed(gain_row), fixed(weights), fixed(spreader)],
        out_specs=[block(NB + LANES)] + [block(columns)] * 3,
        out_shape=[jax.ShapeDtypeStruct((length, NB + LANES), F32), head, head, head],
        name="heads_forward",
    )(tokens, gain_row, weights, spreader)


def heads_backward(factors, spreader, grad_q, grad_k, grad_v):
    length, columns = grad_q.shape
    rows = min(HEAD_ROWS, length)
    block = lambda n: pl.BlockSpec((rows, n), lambda i: (i, 0))
    return pl.pallas_call(
        heads_backward_kernel,
        grid=(length // rows,),
        in_specs=[
            block(NB + LANES), pl.BlockSpec(spreader.shape, lambda i: (0, 0)),
            block(columns), block(columns), block(columns),
        ],
        out_specs=block(NB + LANES),
        out_shape=jax.ShapeDtypeStruct((length, NB + LANES), BF16),
        name="heads_backward",
    )(factors, spreader, grad_q, grad_k, grad_v)


MESH_ID = pl.DeviceIdType.MESH


def place(count):
    me = lax.axis_index("fsdp")
    line, side, core = me // 4, (me // 2) % 2, me % 2
    return me, line, side, core, count // 4


def spot(line, side, core):
    return (line * 2 + side) * 2 + core


def meet(peers):
    barrier = pltpu.get_barrier_semaphore()
    for peer in peers:
        pl.semaphore_signal(barrier, inc=1, device_id=peer, device_id_type=MESH_ID)
    pl.semaphore_wait(barrier, len(peers))


def gather_kernel(x_ref, o_ref, local_sem, send_sem, recv_sem, *, count):
    me, line, side, core, lines = place(count)
    across = [{"fsdp": spot(lax.rem(line + s, lines), side, core)} for s in range(1, lines)]
    beside, partner = {"fsdp": spot(line, 1 - side, core)}, {"fsdp": spot(line, side, 1 - core)}
    meet(across + [beside, partner])
    sends = []

    def copy(src, shard, slot, peer):
        return pltpu.make_async_remote_copy(
            src_ref=src, dst_ref=o_ref.at[shard], send_sem=send_sem.at[slot],
            recv_sem=recv_sem.at[shard], device_id=peer, device_id_type=MESH_ID,
        )

    def send(src, shard, peer):
        made = copy(src, shard, len(sends), peer)
        made.start()
        sends.append(made)

    def arrive(shard):
        copy(o_ref.at[shard], shard, 0, partner).wait_recv()

    own = pltpu.make_async_copy(x_ref, o_ref.at[me], local_sem)
    own.start()
    for peer in across:
        send(x_ref, me, peer)
    send(x_ref, me, beside)
    send(x_ref, me, partner)
    sources = [lax.rem(line + lines - s, lines) for s in range(1, lines)]
    for source in sources:
        shard = spot(source, side, core)
        arrive(shard)
        send(o_ref.at[shard], shard, beside)
        send(o_ref.at[shard], shard, partner)
    for source in [line] + sources:
        shard = spot(source, 1 - side, core)
        arrive(shard)
        send(o_ref.at[shard], shard, partner)
    for source in [line] + sources:
        arrive(spot(source, side, 1 - core))
        arrive(spot(source, 1 - side, 1 - core))
    own.wait()
    for made in sends:
        made.wait_send()


def gather_packed(values, count):
    lines = count // 4
    full = pl.pallas_call(
        functools.partial(gather_kernel, count=count),
        out_shape=jax.ShapeDtypeStruct((count,) + values.shape, values.dtype),
        in_specs=[pl.BlockSpec(memory_space=pltpu.VMEM)],
        out_specs=pl.BlockSpec(memory_space=pltpu.VMEM),
        scratch_shapes=[
            pltpu.SemaphoreType.DMA,
            pltpu.SemaphoreType.DMA((4 * lines - 1,)),
            pltpu.SemaphoreType.DMA((count,)),
        ],
        compiler_params=pltpu.CompilerParams(collective_id=0, has_side_effects=True),
        name="gather_packed",
    )(values)
    return full


def scatter_kernel(
    fac_ref, out_ref, gains_ref, o_ref, part, core_in, side_in, line_in, mine, sp_in,
    core_send, core_recv, side_send, side_recv, line_send, line_recv, sp_send, sp_recv,
    *, count, shards
):
    me, line, side, core, lines = place(count)
    rank = lax.axis_index("sp")
    rows = o_ref.shape[0]
    across = [{"fsdp": spot(lax.rem(line + s, lines), side, core)} for s in range(1, lines)]
    beside, partner = {"fsdp": spot(line, 1 - side, core)}, {"fsdp": spot(line, side, 1 - core)}
    others = [{"sp": lax.rem(rank + s, shards)} for s in range(1, shards)]
    meet(across + [beside, partner] + others)
    started = []

    def copy(src, dst, send_sem, recv_sem, peer):
        return pltpu.make_async_remote_copy(
            src_ref=src, dst_ref=dst, send_sem=send_sem, recv_sem=recv_sem,
            device_id=peer, device_id_type=MESH_ID,
        )

    def send(*args):
        made = copy(*args)
        made.start()
        started.append(made)

    def load(shard):
        begin = pl.multiple_of(shard * rows, rows)
        return jnp.concatenate(
            [fac_ref[pl.ds(begin, rows), :], out_ref[pl.ds(begin, rows), :], gains_ref[shard]],
            axis=1,
        )

    def from_core(slot):
        copy(part.at[me], core_in.at[slot], core_send.at[slot], core_recv.at[slot], partner).wait_recv()
        return core_in[slot].astype(F32)

    def from_side(slot):
        copy(part.at[me], side_in.at[slot], side_send.at[slot], side_recv.at[slot], beside).wait_recv()
        return side_in[slot].astype(F32)

    targets = [lax.rem(line + s, lines) for s in range(1, lines)] + [line]
    for which in (1 - side, side):
        for target in targets:
            shard = spot(target, which, 1 - core)
            slot = target * 2 + which
            part[shard] = load(shard)
            send(part.at[shard], core_in.at[slot], core_send.at[slot], core_recv.at[slot], partner)
    for target in targets:
        shard = spot(target, 1 - side, core)
        part[shard] = (load(shard).astype(F32) + from_core(target * 2 + 1 - side)).astype(BF16)
        send(part.at[shard], side_in.at[target], side_send.at[target], side_recv.at[target], beside)
    for s, target in enumerate(targets):
        shard = spot(target, side, core)
        total = load(shard).astype(F32) + from_core(target * 2 + side) + from_side(target)
        if s < lines - 1:
            part[shard] = total.astype(BF16)
            send(part.at[shard], line_in.at[s], line_send.at[s], line_recv.at[s], across[s])
    for s in range(lines - 1):
        copy(part.at[me], line_in.at[s], line_send.at[s], line_recv.at[s], across[s]).wait_recv()
        total = total + line_in[s].astype(F32)
    mine[...] = total.astype(BF16)
    for s, peer in enumerate(others):
        send(mine, sp_in.at[s], sp_send.at[s], sp_recv.at[s], peer)
    total = mine[...].astype(F32)
    for s, peer in enumerate(others):
        copy(mine, sp_in.at[s], sp_send.at[s], sp_recv.at[s], peer).wait_recv()
        total = total + sp_in[s].astype(F32)
    o_ref[...] = total
    for made in started:
        made.wait_send()


def scatter_packed(grad_fac, grad_out, grad_gains, count, shards):
    rows = grad_fac.shape[0] // count
    columns = grad_fac.shape[1] + grad_out.shape[1] + grad_gains.shape[2]
    lines = count // 4
    buffer = lambda n: pltpu.VMEM((n, rows, columns), BF16)
    sems = lambda n: pltpu.SemaphoreType.DMA((n,))
    return pl.pallas_call(
        functools.partial(scatter_kernel, count=count, shards=shards),
        out_shape=jax.ShapeDtypeStruct((rows, columns), F32),
        in_specs=[pl.BlockSpec(memory_space=pltpu.VMEM)] * 3,
        out_specs=pl.BlockSpec(memory_space=pltpu.VMEM),
        scratch_shapes=[
            buffer(count), buffer(2 * lines), buffer(lines), buffer(lines - 1),
            pltpu.VMEM((rows, columns), BF16), buffer(shards - 1),
            sems(2 * lines), sems(2 * lines), sems(lines), sems(lines),
            sems(lines - 1), sems(lines - 1), sems(shards - 1), sems(shards - 1),
        ],
        compiler_params=pltpu.CompilerParams(collective_id=1, has_side_effects=True),
        name="scatter_packed",
    )(grad_fac, grad_out, grad_gains)


def gather_shards(values, shards):
    me = lax.axis_index("sp")
    rows = values.shape[0]
    full = jnp.zeros((rows * shards,) + values.shape[1:], values.dtype)
    zeros = (0,) * (values.ndim - 1)
    full = lax.dynamic_update_slice(full, values, (me * rows,) + zeros)
    for shift in range(1, shards):
        part = lax.ppermute(values, "sp", [(i, (i + shift) % shards) for i in range(shards)])
        full = lax.dynamic_update_slice(full, part, (((me - shift) % shards) * rows,) + zeros)
    return full


def sum_shards(values, shards):
    if shards == 2:
        other = lax.ppermute(values, "sp", [(0, 1), (1, 0)])
        return values.astype(F32) + other.astype(F32)
    return lax.psum(values, "sp").astype(F32)


def arrange_factor(w, shards):
    heads = H // shards
    spans = ((0, RQ), (H * RQ, RK), (H * (RQ + RK), RK))
    parts = [w[:, H * RANKS :]]
    for device in range(shards):
        own = [
            w[:, base + device * heads * r : base + (device + 1) * heads * r] for base, r in spans
        ]
        parts.append(jnp.pad(jnp.concatenate(own, axis=1), ((0, 0), (0, LANES - heads * RANKS))))
    return jnp.concatenate(parts, axis=1)


def restore_factor(g, shards):
    heads = H // shards
    spans = ((0, RQ), (heads * RQ, RK), (heads * (RQ + RK), RK))
    parts = []
    for base, r in spans:
        for device in range(shards):
            begin = NB + device * LANES + base
            parts.append(g[:, begin : begin + heads * r])
    parts.append(g[:, :NB])
    return jnp.concatenate(parts, axis=1)


def local(tokens, segments, cotangent, gain_attn, w_fac, w_out, gain_ffn, w_gu, w_down, shards, count):
    me = lax.axis_index("sp")
    features = tokens.shape[2]
    heads = H // shards
    columns = heads * DH
    fac_columns = NB + shards * LANES
    own_rows = w_fac.shape[0]

    gains = jnp.concatenate([gain_attn, gain_ffn])[None]
    gains = jnp.pad(gains, ((0, own_rows - 1), (0, LANES - 2 * own_rows)))
    packed = jnp.concatenate([arrange_factor(w_fac, shards), w_out, gains], axis=1)
    packed = gather_packed(packed, count)
    gu_full = lax.all_gather(w_gu, "fsdp", axis=0, tiled=True)
    down_full = lax.all_gather(w_down, "fsdp", axis=0, tiled=True)
    gains = packed[:, 0, fac_columns + features :].astype(F32)
    gain_one = gains[:, :own_rows].reshape(1, features)
    gain_two = gains[:, own_rows : 2 * own_rows].reshape(1, features)
    packed = packed.reshape(features, packed.shape[2])
    fac_full = packed[:, :fac_columns]
    out_full = packed[:, fac_columns : fac_columns + features]

    tokens_all = gather_shards(tokens[0], shards)
    seg_all = gather_shards(segments[0], shards)
    own_left = lax.dynamic_slice_in_dim(fac_full, NB + me * LANES, LANES, 1)
    own_weights = jnp.concatenate([fac_full[:, :NB], own_left], axis=1)
    spreader = expansion(heads)
    factors, query_heads, key_heads, value_heads = heads_forward(
        tokens_all, gain_one, own_weights, spreader, columns
    )
    mixed_heads = attend_forward(query_heads, key_heads, value_heads, seg_all)
    mixed_tokens = lax.all_to_all(mixed_heads, "sp", split_axis=0, concat_axis=1, tiled=True)

    inputs = tokens[0].astype(F32)
    token_count = inputs.shape[0]
    hidden_in = inputs + product(mixed_tokens, out_full)
    normed_two = rms_norm(hidden_in, gain_two).astype(BF16)
    gate_up = product(normed_two, gu_full)
    activated = swiglu(gate_up).astype(BF16)
    grad_out = cotangent[0].astype(F32)
    grad_low = cotangent[0]
    grad_down = weight_grad(activated, grad_low).astype(BF16)
    grad_down = lax.psum_scatter(grad_down, "fsdp", scatter_dimension=0, tiled=True)

    result = hidden_in + product(activated, down_full)
    output = result.astype(BF16)[None]

    grad_act = back_product(grad_low, down_full)
    _, pull_ffn = jax.vjp(swiglu, gate_up)
    grad_gate_up = pull_ffn(grad_act)[0].astype(BF16)
    grad_gu = weight_grad(normed_two, grad_gate_up).astype(BF16)
    grad_gu = lax.psum_scatter(grad_gu, "fsdp", scatter_dimension=0, tiled=True)
    grad_normed_two = back_product(grad_gate_up, gu_full)
    _, pull_two = jax.vjp(rms_norm, hidden_in, gain_two)
    grad_from_norm, grad_gain_two = pull_two(grad_normed_two)
    grad_hidden = grad_out + grad_from_norm
    grad_branch = grad_hidden.astype(BF16)
    grad_wout = weight_grad(mixed_tokens, grad_branch)
    grad_mixed = back_product(grad_branch, out_full).astype(BF16)
    grad_heads = lax.all_to_all(grad_mixed, "sp", split_axis=1, concat_axis=0, tiled=True)
    grad_q, grad_k, grad_v = attend_backward(
        query_heads, key_heads, value_heads, grad_heads, seg_all
    )
    grad_parts = heads_backward(factors, spreader, grad_q, grad_k, grad_v)
    grad_parts = lax.all_to_all(
        grad_parts.reshape(shards, token_count, NB + LANES), "sp", split_axis=0, concat_axis=0
    )
    grad_right = jnp.sum(grad_parts[:, :, :NB].astype(F32), axis=0).astype(BF16)
    grad_factor = jnp.concatenate(
        [grad_right] + [grad_parts[device, :, NB:] for device in range(shards)], axis=1
    )
    normed_one = rms_norm(inputs, gain_one).astype(BF16)
    grad_fac = weight_grad(normed_one, grad_factor)
    grad_normed_one = back_product(grad_factor, fac_full)
    _, pull_one = jax.vjp(rms_norm, inputs, gain_one)
    grad_in_norm, grad_gain_one = pull_one(grad_normed_one)
    grad_tokens = (grad_hidden + grad_in_norm).reshape(1, token_count, features)

    grad_gains = jnp.concatenate(
        [grad_gain_one.reshape(count, own_rows), grad_gain_two.reshape(count, own_rows)], axis=1
    )
    grad_gains = jnp.pad(
        grad_gains[:, None], ((0, 0), (0, own_rows - 1), (0, LANES - 2 * own_rows))
    )
    grad_packed = scatter_packed(
        grad_fac.astype(BF16), grad_wout.astype(BF16), grad_gains.astype(BF16), count, shards
    )
    grad_down = sum_shards(grad_down, shards)
    grad_gu = sum_shards(grad_gu, shards)
    gain_row = grad_packed[0, fac_columns + features :]
    return (
        output,
        grad_tokens,
        gain_row[:own_rows],
        restore_factor(grad_packed[:, :fac_columns], shards),
        grad_packed[:, fac_columns : fac_columns + features],
        gain_row[own_rows : 2 * own_rows],
        grad_gu,
        grad_down,
    )


def solution(mesh):
    in_specs = (
        P("fsdp", "sp", None),
        P("fsdp", "sp"),
        P("fsdp", "sp", None),
        P("fsdp"),
        P("fsdp", None),
        P("fsdp", None),
        P("fsdp"),
        P("fsdp", None),
        P("fsdp", None),
    )
    out_specs = (
        P("fsdp", "sp", None),
        P("fsdp", "sp", None),
        P("fsdp"),
        P("fsdp", None),
        P("fsdp", None),
        P("fsdp"),
        P("fsdp", None),
        P("fsdp", None),
    )

    def body(*args):
        return local(*args, shards=mesh.shape["sp"], count=mesh.shape["fsdp"])

    return jax.shard_map(body, mesh=mesh, in_specs=in_specs, out_specs=out_specs, check_vma=False)
```

profile of v0, /device:TPU:0, one launch (start us, length us, event | category | flops | bytes accessed | tf_op | source)
XLA Modules:
  0.0 443.3 jit_solution(6972057548390248022)
XLA Ops:
  17.1 47.8 %gather_packed.1 = bf16[16,64,2048]{2,1,0:T(8,128)(2,1)} custom-call(bf16[64,2048]{1,0:T(8,128)(2,1)} %copy-done.8), custom_call_target="tpu_custom_call" | custom-call | tf_op jit(solution)/shard_map/gather_packed/pallas_call | solution.py:357
  79.3 10.7 %heads_forward.1 = (f32[1024,768]{1,0:T(8,128)}, bf16[1024,512]{1,0:T(8,128)(2,1)}, bf16[1024,512]{1,0:T(8,128)(2,1)}, bf16[1024,512]{1,0:T(8,128)(2,1)}) custom-call(bf16[1024,1024]{1,0:T(8,128)(2,1)} %copy-done.2, f32[1,1024]{1,0:T(1,128)} %reshape.89.gain_ref, bf16[1024,768]{1,0:T(8,128)(2,1)} %pad_maximum_fusion.w_ref, bf16[256,5120]{1,0:T(8,128)(2,1)} %fusion.13.e_ref), custom_call_target="tpu_custom_call" | custom-call | tf_op jit(solution)/shard_map/heads_forward/pallas_call | solution.py:263
  90.0 16.8 %attend_forward.1 = bf16[1024,512]{1,0:T(8,128)(2,1)} custom-call(bf16[1024,512]{1,0:T(8,128)(2,1)} %get-tuple-element.15.q_ref, bf16[1024,512]{1,0:T(8,128)(2,1)} %get-tuple-element.16.k_ref, bf16[1024,512]{1,0:T(8,128)(2,1)} %get-tuple-element.17.v_ref, s32[1024,1]{1,0:T(8,128)} %copy.18.segc_ref, s32[1,1024]{1,0:T(1,128)} %bitcast.74), custom_call_target="tpu_custom_call" | custom-call | flops 3221225472 | bytes 4194304 | tf_op jit(solution)/shard_map/attend_forward/pallas_call | solution.py:154
  109.1 3.6 all-to-all-start
  113.1 14.1 %all-to-all-done = bf16[2,512,512]{1,2,0:T(8,128)(2,1)S(1)} async-done(((bf16[2,512,512]{1,2,0:T(8,128)(2,1)}), bf16[2,512,512]{1,2,0:T(8,128)(2,1)S(1)}, u32[]{:S(2)}, u32[]{:S(2)}) %all-to-all-start) | async-done | bytes 1048608 | tf_op jit(solution)/shard_map/all_to_all | solution.py:540
  131.6 14.2 %fusion.71 = f32[512,5632]{1,0:T(8,128)} fusion(bf16[1024,5632]{1,0:T(8,128)(2,1)} %all-gather.3.cloned.1.call-done, f32[512,1024]{1,0:T(8,128)S(1)} %get-tuple-element.48, f32[1024]{0:T(1024)S(1)} %mul.181, f32[512]{0:T(512)S(1)} %fusion.62), kind=kOutput, calls=%fused_computation.128 | convolution fusion | flops 5907152896 | bytes 25171968 | tf_op jit(solution)/shard_map/dot_general | solution.py:36
  145.8 41.2 %all-gather.5.cloned.1.call-done = bf16[2816,1024]{1,0:T(8,128)(2,1)} async-done(((bf16[176,1024]{1,0:T(8,128)(2,1)}), bf16[2816,1024]{1,0:T(8,128)(2,1)}) %all-gather.5.cloned.1.call-update) | async-done | bytes 5767184 | tf_op jit(solution)/shard_map/all_gather | solution.py:523
  187.0 13.1 %fusion.40 = (f32[512,2816]{1,0:T(8,128)}, f32[512,2816]{1,0:T(8,128)}, bf16[512,2816]{1,0:T(8,128)(2,1)}) fusion(f32[512,5632]{1,0:T(8,128)} %fusion.71, bf16[2816,1024]{1,0:T(8,128)(2,1)} %all-gather.5.cloned.1.call-done, bf16[1,512,1024]{2,1,0:T(8,128)(2,1)} %param.11), kind=kOutput, calls=%fused_computation.73 | convolution fusion | flops 2972975104 | bytes 32768000 | tf_op jit(solution)/shard_map/tb,ab->ta/dot_general | solution.py:44
  200.1 13.5 %convolution_convert_fusion = bf16[1024,5632]{1,0:T(8,128)(2,1)} fusion(f32[512,2816]{1,0:T(8,128)} %get-tuple-element.27, f32[512,2816]{1,0:T(8,128)} %get-tuple-element.26, f32[512,1024]{1,0:T(8,128)S(1)} %get-tuple-element.48, f32[1024]{0:T(1024)S(1)} %mul.181, f32[512]{0:T(512)S(1)} %fusion.62), kind=kOutput, calls=%fused_computation.10 | convolution fusion | flops 5918687232 | bytes 25171968 | tf_op jit(solution)/shard_map/ta,tb->ab/dot_general | solution.py:40
  214.2 8.1 %convolution_convert_fusion.1 = bf16[2816,1024]{1,0:T(8,128)(2,1)} fusion(bf16[512,2816]{1,0:T(8,128)(2,1)} %get-tuple-element.28, bf16[1,512,1024]{2,1,0:T(8,128)(2,1)} %param.11), kind=kOutput, calls=%fused_computation.20 | convolution fusion | flops 2955673600 | bytes 9699328 | tf_op jit(solution)/shard_map/ta,tb->ab/dot_general | solution.py:40
  222.7 15.7 %multiply_reduce_fusion = (bf16[1024]{0:T(1024)(128)(2,1)S(1)}, f32[512]{0:T(512)S(1)}, f32[512,1024]{1,0:T(8,128)}) fusion(f32[512,1024]{1,0:T(8,128)S(1)} %get-tuple-element.48, f32[512]{0:T(512)S(1)} %fusion.62, f32[1024]{0:T(1024)S(1)} %mul.181, bf16[1024,5632]{1,0:T(8,128)(2,1)} %all-gather.3.cloned.1.call-done, f32[512,2816]{1,0:T(8,128)} %get-tuple-element.27, ...), kind=kOutput, calls=%fused_computation.48 | convolution fusion | flops 5914491392 | bytes 27273216 | tf_op jit(solution)/shard_map/tb,ab->ta/dot_general | solution.py:44
  244.6 4.6 %all-to-all-start.1 = ((bf16[512,2,512]{2,0,1:T(8,128)(2,1)}), bf16[512,2,512]{2,0,1:T(8,128)(2,1)}, u32[]{:S(2)}, u32[]{:S(2)}) async-start(bf16[512,2,512]{2,0,1:T(8,128)(2,1)} %bitcast.67), calls=%async_computation.1 | async-start | bytes 2097152 | tf_op jit(solution)/shard_map/all_to_all | solution.py:568
  249.3 3.9 convolution_convert_fusion.2.out_ref
  253.2 10.4 %all-to-all-done.1 = bf16[512,2,512]{2,0,1:T(8,128)(2,1)} async-done(((bf16[512,2,512]{2,0,1:T(8,128)(2,1)}), bf16[512,2,512]{2,0,1:T(8,128)(2,1)}, u32[]{:S(2)}, u32[]{:S(2)}) %all-to-all-start.1) | async-done | bytes 1048608 | tf_op jit(solution)/shard_map/all_to_all | solution.py:568
  263.6 25.0 %attend_backward.1 = (bf16[1024,512]{1,0:T(8,128)(2,1)}, bf16[1024,512]{1,0:T(8,128)(2,1)}, bf16[1024,512]{1,0:T(8,128)(2,1)}) custom-call(bf16[1024,512]{1,0:T(8,128)(2,1)} %get-tuple-element.15.q_ref, bf16[1024,512]{1,0:T(8,128)(2,1)} %get-tuple-element.16.k_ref, bf16[1024,512]{1,0:T(8,128)(2,1)} %get-tuple-element.17.v_ref, ...), custom_call_target="tpu_custom_call" | custom-call | flops 8053063680 | bytes 7340032 | tf_op jit(solution)/shard_map/attend_backward/pallas_call | solution.py:172
  288.6 12.9 %heads_backward.1 = bf16[1024,768]{1,0:T(8,128)(2,1)} custom-call(f32[1024,768]{1,0:T(8,128)} %get-tuple-element.18.f_ref, bf16[256,5120]{1,0:T(8,128)(2,1)} %fusion.13.e_ref, bf16[1024,512]{1,0:T(8,128)(2,1)} %get-tuple-element.19.dq_ref, bf16[1024,512]{1,0:T(8,128)(2,1)} %get-tuple-element.20.dk_ref, bf16[1024,512]{1,0:T(8,128)(2,1)} %get-tuple-element.21.dv_ref), custom_call_target="tpu_custom_call" | custom-call | tf_op jit(solution)/shard_map/heads_backward/pallas_call | solution.py:277
  301.5 4.8 %all-to-all-start.2 = ((bf16[2,512,768]{2,1,0:T(8,128)(2,1)}), bf16[2,512,768]{2,1,0:T(8,128)(2,1)}, u32[]{:S(2)}, u32[]{:S(2)}) async-start(bf16[2,512,768]{2,1,0:T(8,128)(2,1)} %bitcast.66), calls=%async_computation.2 | async-start | bytes 3145728 | tf_op jit(solution)/shard_map/all_to_all | solution.py:573
  306.3 8.2 %fusion.32 = bf16[1,512,1024]{2,1,0:T(8,128)(2,1)} fusion(f32[512,1024]{1,0:T(8,128)} %copy-done.3, bf16[512,2816]{1,0:T(8,128)(2,1)} %get-tuple-element.28, bf16[2816,1024]{1,0:T(8,128)(2,1)} %all-gather.5.cloned.1.call-done), kind=kOutput, calls=%fused_computation.62 | convolution fusion | flops 2953838592 | bytes 11796480 | tf_op jit(solution)/shard_map/dot_general | solution.py:36
  314.5 10.9 %all-to-all-done.2 = bf16[2,512,768]{2,1,0:T(8,128)(2,1)} async-done(((bf16[2,512,768]{2,1,0:T(8,128)(2,1)}), bf16[2,512,768]{2,1,0:T(8,128)(2,1)}, u32[]{:S(2)}, u32[]{:S(2)}) %all-to-all-start.2) | async-done | bytes 1572896 | tf_op jit(solution)/shard_map/all_to_all | solution.py:573
  328.3 4.3 fusion.17
  333.5 3.7 convolution_convert_fusion.3.fac_ref
  337.2 44.3 %scatter_packed.1 = f32[64,2048]{1,0:T(8,128)} custom-call(bf16[1024,896]{1,0:T(8,128)(2,1)} %convolution_convert_fusion.3.fac_ref, bf16[1024,1024]{1,0:T(8,128)(2,1)} %convolution_convert_fusion.2.out_ref, bf16[16,64,128]{2,1,0:T(8,128)(2,1)} %pad.27.gains_ref), custom_call_target="tpu_custom_call" | custom-call | tf_op jit(solution)/shard_map/scatter_packed/pallas_call | solution.py:451
  389.5 34.5 %reduce-scatter.5.cloned.1.call-done = bf16[176,1024]{1,0:T(8,128)(2,1)} async-done(((bf16[2816,1024]{1,0:T(8,128)(2,1)}), bf16[176,1024]{1,0:T(8,128)(2,1)}) %reduce-scatter.5.cloned.1.call-update) | async-done | bytes 360464 | tf_op jit(solution)/shard_map/reduce_scatter | solution.py:551
  429.0 4.2 collective-permute-done.3
  (97 shorter events, 58.3 us)
Async XLA Ops:
  7.2 124.4 %all-gather.3.cloned.1.call-start = ((), (), s32[]{:S(2)}) async-start(), calls=%async_computation.5 | async-start | bytes 12255232 | tf_op jit(solution)/shard_map/all_gather | solution.py:522
  7.9 179.1 %all-gather.5.cloned.1.call-start = ((), (), s32[]{:S(2)}) async-start(), calls=%async_computation.6 | async-start | bytes 6127616 | tf_op jit(solution)/shard_map/all_gather | solution.py:523
  8.7 66.7 %collective-permute-start.1 = (s32[512]{0:T(512)}, s32[512]{0:T(512)S(1)}, u32[]{:S(2)}, u32[]{:S(2)}) collective-permute-start(s32[512]{0:T(512)} %bitcast.76), channel_id=1, source_target_pairs={{0,16},{16,0},{1,17},{17,1},{2,18},{18,2},{3,19},{19,3},{4,20},{20... | collective-permute-start | bytes 6152 | tf_op jit(solution)/shard_map/ppermute | solution.py:474
  11.7 64.9 %collective-permute-start = (bf16[512,1024]{1,0:T(8,128)(2,1)}, bf16[512,1024]{1,0:T(8,128)(2,1)}, u32[]{:S(2)}, u32[]{:S(2)}) collective-permute-start(bf16[512,1024]{1,0:T(8,128)(2,1)} %bitcast.65), channel_id=1, source_target_pairs={{0,16},{16,0},{1,17},{17,1},{2,18},{18,2},{3,19},{19,3},{4,20},{20... | collective-permute-start | bytes 3145736 | tf_op jit(solution)/shard_map/ppermute | solution.py:474
  16.4 0.7 copy-start.8
  69.1 1.3 copy-start.1
  70.3 2.9 copy-start.4
  73.2 1.3 copy-start.11
  75.6 14.4 %copy-start.10 = (s32[1024]{0:T(1024)}, s32[1024]{0:T(1024)S(1)}, u32[]{:S(2)}) copy-start(s32[1024]{0:T(1024)S(1)} %dynamic_update_slice.15) | copy-start | bytes 12292
  77.9 1.3 copy-start.2
  109.1 18.1 %all-to-all-start = ((bf16[2,512,512]{1,2,0:T(8,128)(2,1)}), bf16[2,512,512]{1,2,0:T(8,128)(2,1)S(1)}, u32[]{:S(2)}, u32[]{:S(2)}) async-start(bf16[2,512,512]{1,2,0:T(8,128)(2,1)} %copy.19), calls=%async_computation | async-start | bytes 2097152 | tf_op jit(solution)/shard_map/all_to_all | solution.py:540
  112.7 270.5 %reduce-scatter.3.cloned.1.call-start = ((), (), s32[]{:S(2)}) async-start(), calls=%async_computation.7 | async-start | bytes 12255232 | tf_op jit(solution)/shard_map/reduce_scatter | solution.py:560
  127.2 1.0 copy-start.5
  131.5 91.2 %copy-start.3 = (f32[512,1024]{1,0:T(8,128)}, f32[512,1024]{1,0:T(8,128)S(1)}, u32[]{:S(2)}) copy-start(f32[512,1024]{1,0:T(8,128)S(1)} %get-tuple-element.48) | copy-start | bytes 6291460
  213.6 210.4 %reduce-scatter.5.cloned.1.call-start = ((), (), s32[]{:S(2)}) async-start(), calls=%async_computation.8 | async-start | bytes 6127616 | tf_op jit(solution)/shard_map/reduce_scatter | solution.py:551
  238.4 3.8 copy-start
  244.6 19.0 %all-to-all-start.1 = ((bf16[512,2,512]{2,0,1:T(8,128)(2,1)}), bf16[512,2,512]{2,0,1:T(8,128)(2,1)}, u32[]{:S(2)}, u32[]{:S(2)}) async-start(bf16[512,2,512]{2,0,1:T(8,128)(2,1)} %bitcast.67), calls=%async_computation.1 | async-start | bytes 2097152 | tf_op jit(solution)/shard_map/all_to_all | solution.py:568
  301.5 24.0 %all-to-all-start.2 = ((bf16[2,512,768]{2,1,0:T(8,128)(2,1)}), bf16[2,512,768]{2,1,0:T(8,128)(2,1)}, u32[]{:S(2)}, u32[]{:S(2)}) async-start(bf16[2,512,768]{2,1,0:T(8,128)(2,1)} %bitcast.66), calls=%async_computation.2 | async-start | bytes 3145728 | tf_op jit(solution)/shard_map/all_to_all | solution.py:573
  327.0 5.5 %copy-start.7 = (bf16[512,640]{1,0:T(8,128)(2,1)}, bf16[512,640]{1,0:T(8,128)(2,1)S(1)}, u32[]{:S(2)}) copy-start(bf16[512,640]{1,0:T(8,128)(2,1)S(1)} %slice_reduce_fusion) | copy-start | bytes 1966084
  383.2 51.0 %collective-permute-start.2 = (bf16[64,5632]{1,0:T(8,128)(2,1)}, bf16[64,5632]{1,0:T(8,128)(2,1)}, u32[]{:S(2)}, u32[]{:S(2)}) collective-permute-start(bf16[64,5632]{1,0:T(8,128)(2,1)} %reduce-scatter.3.cloned.1.call-done), channel_id=1, source_target_pairs={{0,16},{16,0},{1,17},{17,1},{2,18},{18,2},{3,19},{19,3},{4,20},{20... | collective-permute-start | bytes 2162696 | tf_op jit(solution)/shard_map/ppermute | solution.py:481
  424.0 9.2 %collective-permute-start.3 = (bf16[176,1024]{1,0:T(8,128)(2,1)}, bf16[176,1024]{1,0:T(8,128)(2,1)S(1)}, u32[]{:S(2)}, u32[]{:S(2)}) collective-permute-start(bf16[176,1024]{1,0:T(8,128)(2,1)} %reduce-scatter.5.cloned.1.call-done), channel_id=1, source_target_pairs={{0,16},{16,0},{1,17},{17,1},{2,18},{18,2},{3,19},{19,3},{4,20},{20... | collective-permute-start | bytes 1081352 | tf_op jit(solution)/shard_map/ppermute | solution.py:481
  425.4 7.8 %copy-start.9 = (bf16[176,1024]{1,0:T(8,128)(2,1)S(1)}, bf16[176,1024]{1,0:T(8,128)(2,1)}, u32[]{:S(2)}) copy-start(bf16[176,1024]{1,0:T(8,128)(2,1)} %reduce-scatter.5.cloned.1.call-done) | copy-start | bytes 1081348
  425.4 8.7 %copy-start.6 = (bf16[64,5632]{1,0:T(8,128)(2,1)S(1)}, bf16[64,5632]{1,0:T(8,128)(2,1)}, u32[]{:S(2)}) copy-start(bf16[64,5632]{1,0:T(8,128)(2,1)} %reduce-scatter.3.cloned.1.call-done) | copy-start | bytes 2162692
Sparse Core Ops, SparseCore 0:
  10.3 117.4 all-gather.2
  130.0 56.8 all-gather.4
  213.7 125.6 reduce-scatter.2
  343.2 80.7 reduce-scatter.4
where the time goes:
time: 449 us; the launch traced here: 443 us
  Pallas kernels  157 us (35%)
  waiting for transfers between devices  117 us (26%)
  matrix products  89.4 us (20%)
  local copies, waits for them, and re-layouts  27.4 us (6%)
  starting transfers between devices  20.1 us (4%)
  other arithmetic  17.8 us (4%)
  between operations  14.3 us (3%)
    pallas_call x1, Pallas kernels, gather_packed(): pl.pallas_call(functools.partial(gather_kernel, count=count), out_shape=j...  47.8 us
    pallas_call x1, Pallas kernels, scatter_packed(): pl.pallas_call(functools.partial(scatter_kernel, count=count, shards=shar...  44.3 us
    all_gather x1, waiting for transfers between devices, local(): down_full = lax.all_gather(w_down, 'fsdp', axis=0, tiled=True)  41.2 us
    reduce_scatter x1, waiting for transfers between devices, local(): lax.psum_scatter(grad_down, 'fsdp', scatter_dimension=0, tiled=True)  34.5 us
    dot_general x4, matrix products, back_product(): jnp.einsum('tb,ab->ta', grad_rows, weight, preferred_element_type=F32)  34.4 us
    dot_general x4, matrix products, weight_grad(): return jnp.einsum('ta,tb->ab', left, right, preferred_element_type=F32)  29.2 us
    dot_general x3, matrix products, product(): return jnp.dot(left, right, preferred_element_type=F32)  25.7 us
    pallas_call x1, Pallas kernels, attend_backward(): pl.pallas_call(functools.partial(attend_backward_kernel, block=block, wid...  25 us
  transfers between devices with their start and end apart: 11, of which 6 were waited for; matrix products, arithmetic and copies ran while one was open for 23% of the time, Pallas kernels for 36%

commit v1 on v0

--- a/solution.py
+++ b/solution.py
@@ -16,6 +16,7 @@
 LANES = 128
 NB = (RQ + 2 * RK) * DH
 RANKS = RQ + 2 * RK
+MOVED = 768
 
 EPSILON = 1e-06
 NEG = -1e30
@@ -371,7 +372,7 @@
 
 
 def scatter_kernel(
-    fac_ref, out_ref, gains_ref, o_ref, part, core_in, side_in, line_in, mine, sp_in,
+    fac_ref, out_ref, rest_ref, gains_ref, o_ref, part, core_in, side_in, line_in, mine, sp_in,
     core_send, core_recv, side_send, side_recv, line_send, line_recv, sp_send, sp_recv,
     *, count, shards
 ):
@@ -398,7 +399,8 @@
     def load(shard):
         begin = pl.multiple_of(shard * rows, rows)
         return jnp.concatenate(
-            [fac_ref[pl.ds(begin, rows), :], out_ref[pl.ds(begin, rows), :], gains_ref[shard]],
+            [ref[pl.ds(begin, rows), :] for ref in (fac_ref, out_ref, rest_ref)]
+            + [gains_ref[shard]],
             axis=1,
         )
 
@@ -442,16 +444,16 @@
         made.wait_send()
 
 
-def scatter_packed(grad_fac, grad_out, grad_gains, count, shards):
+def scatter_packed(grad_fac, grad_out, grad_rest, grad_gains, count, shards):
     rows = grad_fac.shape[0] // count
-    columns = grad_fac.shape[1] + grad_out.shape[1] + grad_gains.shape[2]
+    columns = sum(a.shape[-1] for a in (grad_fac, grad_out, grad_rest, grad_gains))
     lines = count // 4
     buffer = lambda n: pltpu.VMEM((n, rows, columns), BF16)
     sems = lambda n: pltpu.SemaphoreType.DMA((n,))
     return pl.pallas_call(
         functools.partial(scatter_kernel, count=count, shards=shards),
         out_shape=jax.ShapeDtypeStruct((rows, columns), F32),
-        in_specs=[pl.BlockSpec(memory_space=pltpu.VMEM)] * 3,
+        in_specs=[pl.BlockSpec(memory_space=pltpu.VMEM)] * 4,
         out_specs=pl.BlockSpec(memory_space=pltpu.VMEM),
         scratch_shapes=[
             buffer(count), buffer(2 * lines), buffer(lines), buffer(lines - 1),
@@ -461,7 +463,7 @@
         ],
         compiler_params=pltpu.CompilerParams(collective_id=1, has_side_effects=True),
         name="scatter_packed",
-    )(grad_fac, grad_out, grad_gains)
+    )(grad_fac, grad_out, grad_rest, grad_gains)
 
 
 def gather_shards(values, shards):
@@ -545,6 +547,7 @@
     normed_two = rms_norm(hidden_in, gain_two).astype(BF16)
     gate_up = product(normed_two, gu_full)
     activated = swiglu(gate_up).astype(BF16)
+    gate_up, activated = lax.optimization_barrier((gate_up, activated))
     grad_out = cotangent[0].astype(F32)
     grad_low = cotangent[0]
     grad_down = weight_grad(activated, grad_low).astype(BF16)
@@ -556,7 +559,9 @@
     grad_act = back_product(grad_low, down_full)
     _, pull_ffn = jax.vjp(swiglu, gate_up)
     grad_gate_up = pull_ffn(grad_act)[0].astype(BF16)
-    grad_gu = weight_grad(normed_two, grad_gate_up).astype(BF16)
+    kept = grad_gate_up.shape[1] - MOVED
+    grad_rest = weight_grad(normed_two, grad_gate_up[:, kept:]).astype(BF16)
+    grad_gu = weight_grad(normed_two, grad_gate_up[:, :kept]).astype(BF16)
     grad_gu = lax.psum_scatter(grad_gu, "fsdp", scatter_dimension=0, tiled=True)
     grad_normed_two = back_product(grad_gate_up, gu_full)
     _, pull_two = jax.vjp(rms_norm, hidden_in, gain_two)
@@ -591,11 +596,14 @@
         grad_gains[:, None], ((0, 0), (0, own_rows - 1), (0, LANES - 2 * own_rows))
     )
     grad_packed = scatter_packed(
-        grad_fac.astype(BF16), grad_wout.astype(BF16), grad_gains.astype(BF16), count, shards
+        grad_fac.astype(BF16), grad_wout.astype(BF16), grad_rest, grad_gains.astype(BF16),
+        count, shards,
     )
     grad_down = sum_shards(grad_down, shards)
     grad_gu = sum_shards(grad_gu, shards)
-    gain_row = grad_packed[0, fac_columns + features :]
+    tail = fac_columns + features
+    gain_row = grad_packed[0, tail + MOVED :]
+    grad_gu = jnp.concatenate([grad_gu, grad_packed[:, tail : tail + MOVED]], axis=1)
     return (
         output,
         grad_tokens,

time: 449 us -> 437 us (0.973)
  waiting for transfers between devices: 117 us -> 87.5 us
  Pallas kernels: 157 us -> 177 us
  matrix products: 89.4 us -> 73.1 us
  local copies, waits for them, and re-layouts: 27.4 us -> 39.1 us
    reduce_scatter x1, waiting for transfers between devices: 34.5 us -> 0.02 us  [local(): lax.psum_scatter(grad_down, 'fsdp', scatter_dimension=0, tiled=True)]
    pallas_call x1, Pallas kernels: 44.3 us -> 63.7 us  [scatter_packed(): pl.pallas_call(functools.partial(scatter_kernel, count=count, shards=shar...]
    reduce_scatter x1, waiting for transfers between devices: 0.02 us -> 13.8 us  [local(): grad_gu = lax.psum_scatter(grad_gu, 'fsdp', scatter_dimension=0, tiled=True)]
    all_gather x1, waiting for transfers between devices: 41.2 us -> 31.5 us  [local(): down_full = lax.all_gather(w_down, 'fsdp', axis=0, tiled=True)]
    unnamed x26 -> x36, local copies, waits for them, and re-layouts: 5.53 us -> 13 us
    dot_general x4 -> x5, matrix products: 29.2 us -> 21.8 us  [weight_grad(): return jnp.einsum('ta,tb->ab', left, right, preferred_element_type=F32)]
    dot_general x4, matrix products: 34.4 us -> 29.2 us  [back_product(): jnp.einsum('tb,ab->ta', grad_rows, weight, preferred_element_type=F32)]
    ppermute x2, waiting for transfers between devices: 4.24 us -> 9.07 us  [sum_shards(): other = lax.ppermute(values, 'sp', [(0, 1), (1, 0)])]
  transfers between devices with their start and end apart: 11 -> 11, of which waited for: 6 -> 6; matrix products, arithmetic and copies ran while one was open for 23% -> 28% of each run, Pallas kernels for 36% -> 41%
where the time goes in v1:
time: 437 us; the launch traced here: 431 us
  Pallas kernels  177 us (41%)
  waiting for transfers between devices  87.5 us (20%)
  matrix products  73.1 us (17%)
  local copies, waits for them, and re-layouts  39.1 us (9%)
  starting transfers between devices  21.2 us (5%)
  other arithmetic  19.3 us (4%)
  between operations  14.3 us (3%)
    pallas_call x1, Pallas kernels, scatter_packed(): pl.pallas_call(functools.partial(scatter_kernel, count=count, shards=shar...  63.7 us
    pallas_call x1, Pallas kernels, gather_packed(): pl.pallas_call(functools.partial(gather_kernel, count=count), out_shape=j...  47.8 us
    all_gather x1, waiting for transfers between devices, local(): down_full = lax.all_gather(w_down, 'fsdp', axis=0, tiled=True)  31.5 us
    dot_general x4, matrix products, back_product(): jnp.einsum('tb,ab->ta', grad_rows, weight, preferred_element_type=F32)  29.2 us
    pallas_call x1, Pallas kernels, attend_backward(): pl.pallas_call(functools.partial(attend_backward_kernel, block=block, wid...  25.1 us
    dot_general x3, matrix products, product(): return jnp.dot(left, right, preferred_element_type=F32)  22 us
    dot_general x5, matrix products, weight_grad(): return jnp.einsum('ta,tb->ab', left, right, preferred_element_type=F32)  21.8 us
    pallas_call x1, Pallas kernels, attend_forward(): pl.pallas_call(functools.partial(attend_forward_kernel, block=block, widt...  16.8 us
  transfers between devices with their start and end apart: 11, of which 6 were waited for; matrix products, arithmetic and copies ran while one was open for 28% of the time, Pallas kernels for 41%

profile of v1, /device:TPU:0, one launch (start us, length us, event | category | flops | bytes accessed | tf_op | source)
XLA Modules:
  0.0 431.3 jit_solution(8517824078858655791)
XLA Ops:
  17.1 47.8 %gather_packed.1 = bf16[16,64,2048]{2,1,0:T(8,128)(2,1)} custom-call(bf16[64,2048]{1,0:T(8,128)(2,1)} %copy-done.13), custom_call_target="tpu_custom_call" | custom-call | tf_op jit(solution)/shard_map/gather_packed/pallas_call | solution.py:358
  82.1 10.7 %heads_forward.1 = (f32[1024,768]{1,0:T(8,128)}, bf16[1024,512]{1,0:T(8,128)(2,1)}, bf16[1024,512]{1,0:T(8,128)(2,1)}, bf16[1024,512]{1,0:T(8,128)(2,1)}) custom-call(bf16[1024,1024]{1,0:T(8,128)(2,1)} %constant_dynamic-update-slice_fusion.1.x_ref, f32[1,1024]{1,0:T(1,128)} %reshape.89.gain_ref, bf16[1024,768]{1,0:T(8,128)(2,1)} %pad_maximum_fusion.w_ref, ...), custom_call_target="tpu_custom_call" | custom-call | tf_op jit(solution)/shard_map/heads_forward/pallas_call | solution.py:264
  92.8 16.8 %attend_forward.1 = bf16[1024,512]{1,0:T(8,128)(2,1)} custom-call(bf16[1024,512]{1,0:T(8,128)(2,1)} %get-tuple-element.17.q_ref, bf16[1024,512]{1,0:T(8,128)(2,1)} %get-tuple-element.18.k_ref, bf16[1024,512]{1,0:T(8,128)(2,1)} %get-tuple-element.19.v_ref, s32[1024,1]{1,0:T(8,128)} %copy.18.segc_ref, s32[1,1024]{1,0:T(1,128)} %bitcast.77), custom_call_target="tpu_custom_call" | custom-call | flops 3221225472 | bytes 4194304 | tf_op jit(solution)/shard_map/attend_forward/pallas_call | solution.py:155
  111.9 3.6 all-to-all-start
  115.9 14.0 %all-to-all-done = bf16[2,512,512]{1,2,0:T(8,128)(2,1)S(1)} async-done(((bf16[2,512,512]{1,2,0:T(8,128)(2,1)}), bf16[2,512,512]{1,2,0:T(8,128)(2,1)S(1)}, u32[]{:S(2)}, u32[]{:S(2)}) %all-to-all-start) | async-done | bytes 1048608 | tf_op jit(solution)/shard_map/all_to_all | solution.py:542
  134.8 9.3 %fusion.76 = f32[512,5632]{1,0:T(8,128)S(1)} fusion(bf16[512,1024]{1,0:T(8,128)(2,1)S(1)} %multiply_convert_fusion, bf16[1024,5632]{1,0:T(8,128)(2,1)} %all-gather.3.cloned.1.call-done), kind=kOutput, calls=%fused_computation.138 | convolution fusion | flops 5905580032 | bytes 24117248 | tf_op jit(solution)/shard_map/dot_general | solution.py:37
  149.9 5.0 %convolution_convert_fusion.1 = bf16[2816,1024]{1,0:T(8,128)(2,1)} fusion(bf16[512,2816]{1,0:T(8,128)(2,1)S(1)} %fusion.3, bf16[1,512,1024]{2,1,0:T(8,128)(2,1)S(1)} %copy-done.11), kind=kOutput, calls=%fused_computation.23 | convolution fusion | flops 2955673600 | bytes 9699328 | tf_op jit(solution)/shard_map/ta,tb->ab/dot_general | solution.py:41
  155.5 31.5 %all-gather.5.cloned.1.call-done = bf16[2816,1024]{1,0:T(8,128)(2,1)} async-done(((bf16[176,1024]{1,0:T(8,128)(2,1)}), bf16[2816,1024]{1,0:T(8,128)(2,1)}) %all-gather.5.cloned.1.call-update) | async-done | bytes 5767184 | tf_op jit(solution)/shard_map/all_gather | solution.py:525
  187.0 9.7 %multiply_multiply_fusion = (f32[512,2816]{1,0:T(8,128)S(1)}, f32[512,2816]{1,0:T(8,128)S(1)}) fusion(f32[512,5632]{1,0:T(8,128)} %copy-done.3, bf16[2816,1024]{1,0:T(8,128)(2,1)} %all-gather.5.cloned.1.call-done, bf16[1,512,1024]{2,1,0:T(8,128)(2,1)} %param.11), kind=kOutput, calls=%fused_computation.21 | convolution fusion | flops 2970091520 | bytes 29884416 | tf_op jit(solution)/shard_map/tb,ab->ta/dot_general | solution.py:45
  201.2 7.9 %convolution_convert_fusion = bf16[1024,4864]{1,0:T(8,128)(2,1)} fusion(bf16[512,1024]{1,0:T(8,128)(2,1)S(1)} %multiply_convert_fusion, f32[512,2816]{1,0:T(8,128)S(1)} %get-tuple-element.31, f32[512,2816]{1,0:T(8,128)S(1)} %get-tuple-element.30), kind=kOutput, calls=%fused_computation.11 | convolution fusion | flops 5110235136 | bytes 22544384 | tf_op jit(solution)/shard_map/ta,tb->ab/dot_general | solution.py:41
  209.5 14.0 %multiply_reduce_fusion = (bf16[1024]{0:T(1024)(128)(2,1)S(1)}, f32[512]{0:T(512)S(1)}, f32[512,1024]{1,0:T(8,128)}) fusion(f32[512,1024]{1,0:T(8,128)} %copy-done.5, f32[512]{0:T(512)S(1)} %fusion.61, f32[1024]{0:T(1024)S(1)} %mul.183, bf16[1024,5632]{1,0:T(8,128)(2,1)} %all-gather.3.cloned.1.call-done, f32[512,2816]{1,0:T(8,128)} %copy-done.1, ...), kind=kOutput, calls=%fused_computation.51 | convolution fusion | flops 5914491392 | bytes 27273216 | tf_op jit(solution)/shard_map/tb,ab->ta/dot_general | solution.py:45
  229.7 4.6 %all-to-all-start.1 = ((bf16[512,2,512]{2,0,1:T(8,128)(2,1)}), bf16[512,2,512]{2,0,1:T(8,128)(2,1)}, u32[]{:S(2)}, u32[]{:S(2)}) async-start(bf16[512,2,512]{2,0,1:T(8,128)(2,1)} %bitcast.70), calls=%async_computation.1 | async-start | bytes 2097152 | tf_op jit(solution)/shard_map/all_to_all | solution.py:573
  234.3 3.8 convolution_convert_fusion.4.rest_ref
  240.7 8.0 %all-to-all-done.1 = bf16[512,2,512]{2,0,1:T(8,128)(2,1)} async-done(((bf16[512,2,512]{2,0,1:T(8,128)(2,1)}), bf16[512,2,512]{2,0,1:T(8,128)(2,1)}, u32[]{:S(2)}, u32[]{:S(2)}) %all-to-all-start.1) | async-done | bytes 1048608 | tf_op jit(solution)/shard_map/all_to_all | solution.py:573
  248.7 25.1 %attend_backward.1 = (bf16[1024,512]{1,0:T(8,128)(2,1)}, bf16[1024,512]{1,0:T(8,128)(2,1)}, bf16[1024,512]{1,0:T(8,128)(2,1)}) custom-call(bf16[1024,512]{1,0:T(8,128)(2,1)} %get-tuple-element.17.q_ref, bf16[1024,512]{1,0:T(8,128)(2,1)} %get-tuple-element.18.k_ref, bf16[1024,512]{1,0:T(8,128)(2,1)} %get-tuple-element.19.v_ref, ...), custom_call_target="tpu_custom_call" | custom-call | flops 8053063680 | bytes 7340032 | tf_op jit(solution)/shard_map/attend_backward/pallas_call | solution.py:173
  273.8 12.7 %heads_backward.1 = bf16[1024,768]{1,0:T(8,128)(2,1)} custom-call(f32[1024,768]{1,0:T(8,128)} %get-tuple-element.22.f_ref, bf16[256,5120]{1,0:T(8,128)(2,1)} %fusion.14.e_ref, bf16[1024,512]{1,0:T(8,128)(2,1)} %get-tuple-element.23.dq_ref, bf16[1024,512]{1,0:T(8,128)(2,1)} %get-tuple-element.24.dk_ref, bf16[1024,512]{1,0:T(8,128)(2,1)} %get-tuple-element.25.dv_ref), custom_call_target="tpu_custom_call" | custom-call | tf_op jit(solution)/shard_map/heads_backward/pallas_call | solution.py:278
  286.5 4.9 %all-to-all-start.2 = ((bf16[2,512,768]{2,1,0:T(8,128)(2,1)}), bf16[2,512,768]{2,1,0:T(8,128)(2,1)}, u32[]{:S(2)}, u32[]{:S(2)}) async-start(bf16[2,512,768]{2,1,0:T(8,128)(2,1)} %bitcast.69), calls=%async_computation.2 | async-start | bytes 3145728 | tf_op jit(solution)/shard_map/all_to_all | solution.py:578
  291.4 9.4 %fusion.33 = bf16[1,512,1024]{2,1,0:T(8,128)(2,1)} fusion(f32[512,1024]{1,0:T(8,128)} %copy-done.5, bf16[512,2816]{1,0:T(8,128)(2,1)} %copy-done.8, bf16[2816,1024]{1,0:T(8,128)(2,1)} %all-gather.5.cloned.1.call-done), kind=kOutput, calls=%fused_computation.67 | convolution fusion | flops 2953838592 | bytes 11796480 | tf_op jit(solution)/shard_map/dot_general | solution.py:37
  300.8 9.7 %all-to-all-done.2 = bf16[2,512,768]{2,1,0:T(8,128)(2,1)} async-done(((bf16[2,512,768]{2,1,0:T(8,128)(2,1)}), bf16[2,512,768]{2,1,0:T(8,128)(2,1)}, u32[]{:S(2)}, u32[]{:S(2)}) %all-to-all-start.2) | async-done | bytes 1572896 | tf_op jit(solution)/shard_map/all_to_all | solution.py:578
  313.1 4.2 fusion.18
  320.8 63.7 %scatter_packed.1 = f32[64,2816]{1,0:T(8,128)} custom-call(bf16[1024,896]{1,0:T(8,128)(2,1)} %convolution_convert_fusion.3.fac_ref, bf16[1024,1024]{1,0:T(8,128)(2,1)} %convolution_convert_fusion.2.out_ref, bf16[1024,768]{1,0:T(8,128)(2,1)} %convolution_convert_fusion.4.rest_ref, bf16[16,64,128]{2,1,0:T(8,128)(2,1)} %pad.27.gains_ref), custom_call_target="tpu_custom_call" | custom-call | tf_op jit(solution)/shard_map/scatter_packed/pallas_call | solution.py:453
  393.7 13.8 %reduce-scatter.3.cloned.1.call-done = bf16[64,4864]{1,0:T(8,128)(2,1)} async-done(((bf16[1024,4864]{1,0:T(8,128)(2,1)}), bf16[64,4864]{1,0:T(8,128)(2,1)}) %reduce-scatter.3.cloned.1.call-update) | async-done | bytes 622608 | tf_op jit(solution)/shard_map/reduce_scatter | solution.py:565
  409.0 4.2 fusion.21
  414.1 9.1 %collective-permute-done.2 = bf16[64,4864]{1,0:T(8,128)(2,1)S(1)} collective-permute-done((bf16[64,4864]{1,0:T(8,128)(2,1)}, bf16[64,4864]{1,0:T(8,128)(2,1)S(1)}, u32[]{:S(2)}, u32[]{:S(2)}) %collective-permute-start.2) | collective-permute-done | bytes 622624 | tf_op jit(solution)/shard_map/ppermute | solution.py:483
  (113 shorter events, 73.7 us)
Async XLA Ops:
  7.2 127.7 %all-gather.3.cloned.1.call-start = ((), (), s32[]{:S(2)}) async-start(), calls=%async_computation.5 | async-start | bytes 12255232 | tf_op jit(solution)/shard_map/all_gather | solution.py:524
  7.9 179.1 %all-gather.5.cloned.1.call-start = ((), (), s32[]{:S(2)}) async-start(), calls=%async_computation.6 | async-start | bytes 6127616 | tf_op jit(solution)/shard_map/all_gather | solution.py:525
  8.7 69.9 %collective-permute-start.1 = (s32[512]{0:T(512)}, s32[512]{0:T(512)S(1)}, u32[]{:S(2)}, u32[]{:S(2)}) collective-permute-start(s32[512]{0:T(512)} %bitcast.79), channel_id=1, source_target_pairs={{0,16},{16,0},{1,17},{17,1},{2,18},{18,2},{3,19},{19,3},{4,20},{20... | collective-permute-start | bytes 6152 | tf_op jit(solution)/shard_map/ppermute | solution.py:476
  11.7 68.1 %collective-permute-start = (bf16[512,1024]{1,0:T(8,128)(2,1)}, bf16[512,1024]{1,0:T(8,128)(2,1)}, u32[]{:S(2)}, u32[]{:S(2)}) collective-permute-start(bf16[512,1024]{1,0:T(8,128)(2,1)} %bitcast.68), channel_id=1, source_target_pairs={{0,16},{16,0},{1,17},{17,1},{2,18},{18,2},{3,19},{19,3},{4,20},{20... | collective-permute-start | bytes 3145736 | tf_op jit(solution)/shard_map/ppermute | solution.py:476
  66.4 6.4 %copy-start.4 = (bf16[1,512,1024]{2,1,0:T(8,128)(2,1)S(1)}, bf16[1,512,1024]{2,1,0:T(8,128)(2,1)}, u32[]{:S(2)}) copy-start(bf16[1,512,1024]{2,1,0:T(8,128)(2,1)} %param.9) | copy-start | bytes 3145732
  73.8 3.9 copy-start.16
  78.8 14.0 %copy-start.15 = (s32[1024]{0:T(1024)}, s32[1024]{0:T(1024)S(1)}, u32[]{:S(2)}) copy-start(s32[1024]{0:T(1024)S(1)} %dynamic_update_slice.15) | copy-start | bytes 12292
  111.9 18.0 %all-to-all-start = ((bf16[2,512,512]{1,2,0:T(8,128)(2,1)}), bf16[2,512,512]{1,2,0:T(8,128)(2,1)S(1)}, u32[]{:S(2)}, u32[]{:S(2)}) async-start(bf16[2,512,512]{1,2,0:T(8,128)(2,1)} %copy.19), calls=%async_computation | async-start | bytes 2097152 | tf_op jit(solution)/shard_map/all_to_all | solution.py:542
  115.5 275.6 %reduce-scatter.5.cloned.1.call-start = ((), (), s32[]{:S(2)}) async-start(), calls=%async_computation.8 | async-start | bytes 6127616 | tf_op jit(solution)/shard_map/reduce_scatter | solution.py:554
  129.9 3.3 copy-start.9
  144.1 4.2 copy-start.3
  144.1 5.8 %copy-start.11 = (bf16[1,512,1024]{2,1,0:T(8,128)(2,1)S(1)}, bf16[1,512,1024]{2,1,0:T(8,128)(2,1)}, u32[]{:S(2)}) copy-start(bf16[1,512,1024]{2,1,0:T(8,128)(2,1)} %param.11) | copy-start | bytes 3145732
  154.9 252.6 %reduce-scatter.3.cloned.1.call-start = ((), (), s32[]{:S(2)}) async-start(), calls=%async_computation.7 | async-start | bytes 10584064 | tf_op jit(solution)/shard_map/reduce_scatter | solution.py:565
  196.7 4.5 %copy-start.1 = (f32[512,2816]{1,0:T(8,128)}, f32[512,2816]{1,0:T(8,128)S(1)}, u32[]{:S(2)}) copy-start(f32[512,2816]{1,0:T(8,128)S(1)} %get-tuple-element.31) | copy-start | bytes 17301508
  223.5 3.8 copy-start.2
  229.7 19.0 %all-to-all-start.1 = ((bf16[512,2,512]{2,0,1:T(8,128)(2,1)}), bf16[512,2,512]{2,0,1:T(8,128)(2,1)}, u32[]{:S(2)}, u32[]{:S(2)}) async-start(bf16[512,2,512]{2,0,1:T(8,128)(2,1)} %bitcast.70), calls=%async_computation.1 | async-start | bytes 2097152 | tf_op jit(solution)/shard_map/all_to_all | solution.py:573
  234.3 3.8 copy-start.7
  234.3 3.8 copy-start.10
  286.5 24.0 %all-to-all-start.2 = ((bf16[2,512,768]{2,1,0:T(8,128)(2,1)}), bf16[2,512,768]{2,1,0:T(8,128)(2,1)}, u32[]{:S(2)}, u32[]{:S(2)}) async-start(bf16[2,512,768]{2,1,0:T(8,128)(2,1)} %bitcast.69), calls=%async_computation.2 | async-start | bytes 3145728 | tf_op jit(solution)/shard_map/all_to_all | solution.py:578
  391.1 22.1 %collective-permute-start.3 = (bf16[176,1024]{1,0:T(8,128)(2,1)}, bf16[176,1024]{1,0:T(8,128)(2,1)S(1)}, u32[]{:S(2)}, u32[]{:S(2)}) collective-permute-start(bf16[176,1024]{1,0:T(8,128)(2,1)} %reduce-scatter.5.cloned.1.call-done), channel_id=1, source_target_pairs={{0,16},{16,0},{1,17},{17,1},{2,18},{18,2},{3,19},{19,3},{4,20},{20... | collective-permute-start | bytes 1081352 | tf_op jit(solution)/shard_map/ppermute | solution.py:483
  407.5 15.7 %collective-permute-start.2 = (bf16[64,4864]{1,0:T(8,128)(2,1)}, bf16[64,4864]{1,0:T(8,128)(2,1)S(1)}, u32[]{:S(2)}, u32[]{:S(2)}) collective-permute-start(bf16[64,4864]{1,0:T(8,128)(2,1)} %reduce-scatter.3.cloned.1.call-done), channel_id=1, source_target_pairs={{0,16},{16,0},{1,17},{17,1},{2,18},{18,2},{3,19},{19,3},{4,20},{20... | collective-permute-start | bytes 1867784 | tf_op jit(solution)/shard_map/ppermute | solution.py:483
  409.0 4.2 copy-start.14
  409.0 14.2 %copy-start.12 = (bf16[64,4864]{1,0:T(8,128)(2,1)S(1)}, bf16[64,4864]{1,0:T(8,128)(2,1)}, u32[]{:S(2)}) copy-start(bf16[64,4864]{1,0:T(8,128)(2,1)} %reduce-scatter.3.cloned.1.call-done) | copy-start | bytes 1867780
  413.1 10.2 %slice-start = ((f32[64,2816]{1,0:T(8,128)}), f32[64,768]{1,0:T(8,128)S(1)}, s32[]{:S(2)}) async-start(f32[64,2816]{1,0:T(8,128)} %scatter_packed.1), calls=%async_computation.9 | async-start | bytes 393216 | tf_op jit(solution)/shard_map/slice | solution.py:606
  (5 other events, 7.4 us)
Sparse Core Ops, SparseCore 0:
  10.3 117.4 all-gather.2
  130.0 56.8 all-gather.4
  190.9 80.0 reduce-scatter.4
  275.0 132.4 reduce-scatter.2
